TPU v7x, 32 devices: a whole 2x2x4 slice. The times are simulated.
32 devices in a mesh: tile: 16 (over z, x, core), rep: 2 (over y).
Axes of the slice: x: 2, y: 2, z: 4, core: 2. Of those that a mesh axis runs over, the one named last changes fastest.
Arguments:
- waves: bfloat16 [2, 8192, 128], P('rep', 'tile'), may hold values from -6 to 6
- dest_tile: int32 [2, 8192, 1], P('rep', 'tile'), may hold values from 0 to 15; in each aligned block of 512 rows (0 to 511, 512 to 1023, ..., all dimensions but the last counted through in order) at most 32 rows name the same one
- pixel_bin: int32 [2, 8192], P('rep', 'tile'), may hold values from 0 to 1023
- target: float32 [2, 128, 128], P('rep', 'tile'), may hold values from -6 to 6
- conv_one: bfloat16 [3, 3, 128, 128], replicated, may hold values from -0.1875 to 0.1875
- bias_one: float32 [128], replicated, may hold values from -0.5 to 0.5
- conv_two: bfloat16 [3, 3, 128], replicated, may hold values from -0.1875 to 0.1875
- bias_two: float32 [1], replicated, may hold values from -1 to 1
Outputs:
- prediction: float32 [2, 128, 128], P('rep', 'tile')
- update_one: float32 [3, 3, 128, 128], replicated
- update_bias: float32 [128], replicated
- update_two: float32 [3, 3, 128], replicated
Inputs may be any that keep to these rules, and one draw needn't show every extreme that they name: `dest_tile`: among the rows of one device, no strip is named more than 32 times, a bound that some block reaches.
All inputs are finite; a program needn't handle non-finite values.
Results may differ from a plain program's by a relative error of at most 0.0024.
The roundings to bfloat16 on the way count: a program that leaves them out, or rounds other values in their place, can miss the bound.
Values may be sent and summed in bfloat16 or wider, within the bound.
A program may use at most 64 MiB of HBM per device.

v0:
```python
import math
import jax
import jax.numpy as jnp
from jax import lax
from jax.sharding import PartitionSpec as P

CAP = 32


def extended(block, sides, width):
    for axis, dim in sides:
        count = lax.axis_size(axis)
        forward = [(i, i + 1) for i in range(count - 1)]
        backward = [(target, source) for source, target in forward]
        low = lax.ppermute(
            lax.slice_in_dim(block, block.shape[dim] - width, None, axis=dim), axis, forward
        )
        high = lax.ppermute(lax.slice_in_dim(block, 0, width, axis=dim), axis, backward)
        block = jnp.concatenate([low, block, high], axis=dim)
    return block


def normalized(grad):
    return grad / jnp.sqrt(jnp.mean(grad * grad) + 1e-06)


def first_conv(padded, conv_one, bias_one, tall, width):
    steps = padded.shape[2]
    channels = conv_one.shape[3]
    pre = jnp.zeros((tall * width, channels), jnp.float32) + bias_one[None, :]
    for i in range(3):
        for j in range(3):
            patch = padded[2 * i : 2 * i + tall, 2 * j : 2 * j + width, :].reshape(
                tall * width, steps
            )
            pre = pre + jnp.dot(patch, conv_one[i, j], preferred_element_type=jnp.float32)
    return pre.reshape(tall, width, channels)


def second_conv(hidden_pad, conv_two, bias_two, tall, width):
    pred = jnp.zeros((tall, width), jnp.float32) + bias_two[0]
    for i in range(3):
        for j in range(3):
            pred = pred + jnp.einsum(
                "hwc,c->hw",
                hidden_pad[i : i + tall, j : j + width, :],
                conv_two[i, j],
                preferred_element_type=jnp.float32,
            )
    return pred


def on_device(waves, dest_tile, pixel_bin, target, conv_one, bias_one, conv_two, bias_two):
    tiles = lax.axis_size("tile")
    replicas = lax.axis_size("rep")
    steps = waves.shape[2]
    height = target.shape[1]
    width = target.shape[2]
    pixels = height * width
    channels = conv_one.shape[3]
    bucket = CAP
    tile_ids = dest_tile[0, :, 0]
    hits = (tile_ids[:, None] == jnp.arange(tiles, dtype=jnp.int32)[None, :]).astype(jnp.int32)
    rank = jnp.sum(jnp.cumsum(hits, axis=0) * hits, axis=1) - 1
    slots = tile_ids * bucket + rank
    send_wave = jnp.zeros((tiles * bucket, steps), jnp.bfloat16).at[slots].set(waves[0])
    send_bin = jnp.full((tiles * bucket,), -1, jnp.int32).at[slots].set(pixel_bin[0])
    recv_wave, recv_bin = (
        lax.all_to_all(
            send_wave.reshape(tiles, bucket, steps), "tile", split_axis=0, concat_axis=0, tiled=True
        ),
        lax.all_to_all(
            send_bin.reshape(tiles, bucket), "tile", split_axis=0, concat_axis=0, tiled=True
        ),
    )
    recv_wave = recv_wave.reshape(tiles * bucket, steps)
    recv_bin = recv_bin.reshape(tiles * bucket)
    block = math.gcd(pixels, 128)

    def raster(start):
        wanted = start + jnp.arange(block, dtype=jnp.int32)
        onehot = (wanted[:, None] == recv_bin[None, :]).astype(jnp.bfloat16)
        return jnp.dot(onehot, recv_wave, preferred_element_type=jnp.float32).astype(jnp.bfloat16)

    starts = jnp.arange(0, pixels, block, dtype=jnp.int32)
    grid = lax.map(raster, starts)
    padded = extended(grid, (("tile", 0),), 2)
    padded = jnp.pad(padded, ((0, 0), (2, 2), (0, 0)))
    pre = first_conv(padded, conv_one, bias_one, height, width)
    hidden = jax.nn.silu(pre).astype(jnp.bfloat16)
    hidden_pad = extended(hidden, (("tile", 0),), 1)
    hidden_pad = jnp.pad(hidden_pad, ((0, 0), (1, 1), (0, 0)))
    pred = second_conv(hidden_pad, conv_two, bias_two, height, width)
    error = ((pred - target[0]) / replicas).astype(jnp.bfloat16)
    error_pad = extended(error, (("tile", 0),), 1)
    error_pad = jnp.pad(error_pad, ((0, 0), (1, 1)))
    grad_two = []
    back = jnp.zeros((height, width, channels), jnp.float32)
    for i in range(3):
        for j in range(3):
            grad_two.append(
                jnp.einsum(
                    "hwc,hw->c",
                    hidden_pad[i : i + height, j : j + width, :],
                    error,
                    preferred_element_type=jnp.float32,
                )
            )
            shifted = error_pad[2 - i : 2 - i + height, 2 - j : 2 - j + width].astype(jnp.float32)
            back = back + shifted[:, :, None] * conv_two[i, j].astype(jnp.float32)[None, None, :]
    grad_two = jnp.stack(grad_two).reshape(3, 3, channels)
    sig = jax.nn.sigmoid(pre)
    slope = (back * sig * (1.0 + pre * (1.0 - sig))).astype(jnp.bfloat16)
    slope_flat = slope.reshape(pixels, channels)
    grad_one = []
    for i in range(3):
        for j in range(3):
            patch = padded[2 * i : 2 * i + height, 2 * j : 2 * j + width, :].reshape(pixels, steps)
            grad_one.append(
                lax.dot_general(
                    patch, slope_flat, (((0,), (0,)), ((), ())), preferred_element_type=jnp.float32
                )
            )
    grad_one = jnp.stack(grad_one).reshape(3, 3, steps, channels)
    grad_bias = jnp.sum(slope_flat.astype(jnp.float32), axis=0)
    share = lax.psum_scatter(
        grad_one.reshape(9 * steps, channels), "tile", scatter_dimension=0, tiled=True
    )
    share = lax.psum(share, "rep")
    grad_one = lax.all_gather(share, "tile", axis=0, tiled=True).reshape(3, 3, steps, channels)
    grad_bias, grad_two = lax.psum((grad_bias, grad_two), ("tile", "rep"))
    return (pred[None], normalized(grad_one), normalized(grad_bias), normalized(grad_two))


def solution(mesh):
    placed = (
        P("rep", "tile", None),
        P("rep", "tile", None),
        P("rep", "tile"),
        P("rep", "tile", None),
        P(),
        P(),
        P(),
        P(),
    )
    return jax.shard_map(
        on_device,
        mesh=mesh,
        in_specs=placed,
        out_specs=(P("rep", "tile", None), P(), P(), P()),
        check_vma=False,
    )
```

profile of v0, /device:TPU:0, one launch (start us, length us, event | category | flops | bytes accessed | tf_op | source)
XLA Modules:
  0.0 186.0 jit_solution(650408584183058171)
XLA Ops:
  7.9 1.1 reduce-window.6
  10.8 2.6 %scatter_custom_fusion = s32[512]{0:T(512)S(1)} fusion(s32[512]{0:T(512)S(1)} %bitcast.330, s32[512]{0:T(512)} %bitcast.332, s32[]{:T(128)} %constant.22.clone.1), kind=kCustom, calls=%fused_computation.156 | custom fusion | bytes 2560 | tf_op jit(solution)/shard_map/scatter | solution.py:67
  14.1 7.4 %all-to-all-start = ((s32[16,1,32]{2,1,0:T(1,128)}), s32[16,1,32]{2,1,0:T(1,128)S(1)}, u32[]{:S(2)}, u32[]{:S(2)}) async-start(s32[16,1,32]{2,1,0:T(1,128)} %all_to_all.11), calls=%async_computation | async-start | bytes 16384 | tf_op jit(solution)/shard_map/all_to_all | solution.py:72
  21.4 2.4 %scatter_custom_fusion.1 = bf16[512,128]{1,0:T(8,128)(2,1)} fusion(s32[512]{0:T(512)S(1)} %bitcast.331, bf16[1,512,128]{2,1,0:T(8,128)(2,1)S(1)} %copy-done, bf16[]{:T(256)} %constant.14.clone.1), kind=kCustom, calls=%fused_computation.100 | custom fusion | bytes 262146 | tf_op jit(solution)/shard_map/scatter | solution.py:66
  23.8 4.0 %all-to-all-done = s32[16,1,32]{2,1,0:T(1,128)S(1)} async-done(((s32[16,1,32]{2,1,0:T(1,128)}), s32[16,1,32]{2,1,0:T(1,128)S(1)}, u32[]{:S(2)}, u32[]{:S(2)}) %all-to-all-start) | async-done | bytes 2080 | tf_op jit(solution)/shard_map/all_to_all | solution.py:72
  27.8 3.5 %all-to-all-start.1 = ((bf16[16,32,128]{2,1,0:T(8,128)(2,1)}), bf16[16,32,128]{2,1,0:T(8,128)(2,1)S(1)}, u32[]{:S(2)}, u32[]{:S(2)}) async-start(bf16[16,32,128]{2,1,0:T(8,128)(2,1)} %bitcast.12), calls=%async_computation.1 | async-start | bytes 262144 | tf_op jit(solution)/shard_map/all_to_all | solution.py:69
  31.5 7.8 %all-to-all-done.1 = bf16[16,32,128]{2,1,0:T(8,128)(2,1)S(1)} async-done(((bf16[16,32,128]{2,1,0:T(8,128)(2,1)}), bf16[16,32,128]{2,1,0:T(8,128)(2,1)S(1)}, u32[]{:S(2)}, u32[]{:S(2)}) %all-to-all-start.1) | async-done | bytes 131104 | tf_op jit(solution)/shard_map/all_to_all | solution.py:69
  39.3 12.0 %while.11 = (s32[]{:T(128)}, bf16[8,128,128]{2,1,0:T(8,128)(2,1)S(1)}, s32[8]{0:T(128)S(1)}, s32[16,32]{1,0:T(8,128)}, bf16[512,128]{1,0:T(8,128)(2,1)S(1)}, /*index=5*/s32[512]{0:T(512)S(1)}, s32[]{:T(128)}) while((s32[]{:T(128)}, bf16[8,128,128]{2,1,0:T(8,128)(2,1)S(1)}, s32[8]{0:T(128)S(1)}, s32[16,32]{1,0:T(8,128)}, ...), condition=%wide.wide.region_6.7_spmd, body=%wide.wide.region_5.6_spmd.sunk | while | flops 16859264 | bytes 167009 | solution.py:86
  51.5 1.3 collective-permute-start
  52.8 1.3 collective-permute-start.1
  57.6 0.9 pad_maximum_fusion.2
  61.2 1.0 convolution_add_fusion.8
  65.0 4.4 %collective-permute-start.2 = (bf16[1,128,128]{2,1,0:T(8,128)(2,1)S(1)}, bf16[1,128,128]{2,1,0:T(8,128)(2,1)S(1)}, u32[]{:S(2)}, u32[]{:S(2)}) collective-permute-start(bf16[1,128,128]{2,1,0:T(8,128)(2,1)S(1)} %get-tuple-element.53), channel_id=1, source_target_pairs={{0,2},{2,4},{4,6},{6,8},{8,10},{10,12},{12,14},{14,16},{16,18},{18... | collective-permute-start | bytes 98312 | tf_op jit(solution)/shard_map/ppermute | solution.py:15
  69.4 1.3 collective-permute-start.3
  70.8 1.6 collective-permute-done.3
  76.0 4.8 %collective-permute-start.4 = (bf16[1,128]{1,0:T(2,128)(2,1)S(1)}, bf16[1,128]{1,0:T(2,128)(2,1)S(1)}, u32[]{:S(2)}, u32[]{:S(2)}) collective-permute-start(bf16[1,128]{1,0:T(2,128)(2,1)S(1)} %get-tuple-element.87), channel_id=1, source_target_pairs={{0,2},{2,4},{4,6},{6,8},{8,10},{10,12},{12,14},{14,16},{16,18},{18... | collective-permute-start | bytes 776 | tf_op jit(solution)/shard_map/ppermute | solution.py:15
  80.8 1.3 collective-permute-start.5
  82.4 1.4 collective-permute-done.5
  84.0 1.6 multiply_convert_fusion.1
  88.8 1.6 convert_reduce_fusion
  90.5 42.7 %all-reduce.4 = (f32[128]{0:T(128)S(1)}, f32[3,3,128]{2,1,0:T(4,128)S(1)}) all-reduce(f32[128]{0:T(128)S(1)} %convert_reduce_fusion, f32[3,3,128]{2,1,0:T(4,128)S(1)} %reshape.152), channel_id=1, replica_groups=mesh['tile'=16,'rep'=2] {'tile','rep'}, use_global_device_ids=true, to_apply=%region_11.12 | all-reduce | flops 1280 | bytes 10240 | tf_op jit(solution)/shard_map/psum | solution.py:131
  136.9 9.8 %reduce-scatter.4.cloned.1.call-done = f32[72,128]{1,0:T(8,128)} async-done(((f32[1152,128]{1,0:T(8,128)}), f32[72,128]{1,0:T(8,128)}) %reduce-scatter.4.cloned.1.call-update) | async-done | bytes 36880
  146.7 9.1 %psum.21 = f32[72,128]{1,0:T(8,128)S(1)} all-reduce(f32[72,128]{1,0:T(8,128)} %reduce-scatter.4.cloned.1.call-done), channel_id=1, replica_groups=mesh['tile'=16,'rep'=2] {'rep'}, use_global_device_ids=true, to_apply=%region_8.9 | all-reduce | flops 9216 | bytes 73728 | tf_op jit(solution)/shard_map/psum | solution.py:129
  155.8 21.1 %all_gather.3 = f32[1152,128]{1,0:T(8,128)S(1)} all-gather(f32[72,128]{1,0:T(8,128)S(1)} %psum.21), channel_id=1, replica_groups=mesh['tile'=16,'rep'=2] {'tile'}, dimensions={0}, use_global_device_ids=true | all-gather | bytes 626688 | tf_op jit(solution)/shard_map/all_gather | solution.py:130
  (141 shorter events, 34.6 us)
Async XLA Ops:
  7.2 14.3 %copy-start = (bf16[1,512,128]{2,1,0:T(8,128)(2,1)S(1)}, bf16[1,512,128]{2,1,0:T(8,128)(2,1)}, u32[]{:S(2)}) copy-start(bf16[1,512,128]{2,1,0:T(8,128)(2,1)} %param.10) | copy-start | bytes 393220
  14.1 13.8 %all-to-all-start = ((s32[16,1,32]{2,1,0:T(1,128)}), s32[16,1,32]{2,1,0:T(1,128)S(1)}, u32[]{:S(2)}, u32[]{:S(2)}) async-start(s32[16,1,32]{2,1,0:T(1,128)} %all_to_all.11), calls=%async_computation | async-start | bytes 16384 | tf_op jit(solution)/shard_map/all_to_all | solution.py:72
  27.8 11.4 %copy-start.9 = (s32[16,1,32]{2,1,0:T(1,128)}, s32[16,1,32]{2,1,0:T(1,128)S(1)}, u32[]{:S(2)}) copy-start(s32[16,1,32]{2,1,0:T(1,128)S(1)} %all-to-all-done) | copy-start | bytes 6148
  27.8 11.4 %all-to-all-start.1 = ((bf16[16,32,128]{2,1,0:T(8,128)(2,1)}), bf16[16,32,128]{2,1,0:T(8,128)(2,1)S(1)}, u32[]{:S(2)}, u32[]{:S(2)}) async-start(bf16[16,32,128]{2,1,0:T(8,128)(2,1)} %bitcast.12), calls=%async_computation.1 | async-start | bytes 262144 | tf_op jit(solution)/shard_map/all_to_all | solution.py:69
  31.4 115.3 %reduce-scatter.4.cloned.1.call-start = ((), (), s32[]{:S(2)}) async-start(), calls=%async_computation.3 | async-start | bytes 626688
  39.3 14.9 %copy-start.10 = (bf16[3,3,128]{2,1,0:T(4,128)(2,1)S(1)}, bf16[3,3,128]{2,1,0:T(4,128)(2,1)}, u32[]{:S(2)}) copy-start(bf16[3,3,128]{2,1,0:T(4,128)(2,1)} %param.16) | copy-start | bytes 6916
  51.5 3.9 %collective-permute-start = (bf16[2,128,128]{1,2,0:T(8,128)(2,1)S(1)}, bf16[2,128,128]{1,2,0:T(8,128)(2,1)S(1)}, u32[]{:S(2)}, u32[]{:S(2)}) collective-permute-start(bf16[2,128,128]{1,2,0:T(8,128)(2,1)S(1)} %get-tuple-element.57), channel_id=1, source_target_pairs={{0,2},{2,4},{4,6},{6,8},{8,10},{10,12},{12,14},{14,16},{16,18},{18... | collective-permute-start | bytes 196616 | tf_op jit(solution)/shard_map/ppermute | solution.py:15
  52.8 3.1 %collective-permute-start.1 = (bf16[2,128,128]{1,2,0:T(8,128)(2,1)S(1)}, bf16[2,128,128]{1,2,0:T(8,128)(2,1)S(1)}, u32[]{:S(2)}, u32[]{:S(2)}) collective-permute-start(bf16[2,128,128]{1,2,0:T(8,128)(2,1)S(1)} %get-tuple-element.58), channel_id=1, source_target_pairs={{2,0},{4,2},{6,4},{8,6},{10,8},{12,10},{14,12},{16,14},{18,16},{20... | collective-permute-start | bytes 196616 | tf_op jit(solution)/shard_map/ppermute | solution.py:18
  61.0 1.3 copy-start.2
  61.2 1.1 copy-start.8
  62.3 1.0 copy-start.1
  65.0 5.9 %collective-permute-start.2 = (bf16[1,128,128]{2,1,0:T(8,128)(2,1)S(1)}, bf16[1,128,128]{2,1,0:T(8,128)(2,1)S(1)}, u32[]{:S(2)}, u32[]{:S(2)}) collective-permute-start(bf16[1,128,128]{2,1,0:T(8,128)(2,1)S(1)} %get-tuple-element.53), channel_id=1, source_target_pairs={{0,2},{2,4},{4,6},{6,8},{8,10},{10,12},{12,14},{14,16},{16,18},{18... | collective-permute-start | bytes 98312 | tf_op jit(solution)/shard_map/ppermute | solution.py:15
  69.4 3.1 %collective-permute-start.3 = (bf16[1,128,128]{2,1,0:T(8,128)(2,1)S(1)}, bf16[1,128,128]{2,1,0:T(8,128)(2,1)S(1)}, u32[]{:S(2)}, u32[]{:S(2)}) collective-permute-start(bf16[1,128,128]{2,1,0:T(8,128)(2,1)S(1)} %get-tuple-element.54), channel_id=1, source_target_pairs={{2,0},{4,2},{6,4},{8,6},{10,8},{12,10},{14,12},{16,14},{18,16},{20... | collective-permute-start | bytes 98312 | tf_op jit(solution)/shard_map/ppermute | solution.py:18
  75.8 8.2 %copy-start.11 = (f32[128]{0:T(128)S(1)}, f32[128]{0:T(128)}, u32[]{:S(2)}) copy-start(f32[128]{0:T(128)} %get-tuple-element.74) | copy-start | bytes 1540
  75.8 8.2 %copy-start.12 = (f32[128]{0:T(128)S(1)}, f32[128]{0:T(128)}, u32[]{:S(2)}) copy-start(f32[128]{0:T(128)} %get-tuple-element.75) | copy-start | bytes 1540
  75.8 8.2 %copy-start.13 = (f32[128]{0:T(128)S(1)}, f32[128]{0:T(128)}, u32[]{:S(2)}) copy-start(f32[128]{0:T(128)} %get-tuple-element.76) | copy-start | bytes 1540
  75.8 8.2 %copy-start.14 = (f32[128]{0:T(128)S(1)}, f32[128]{0:T(128)}, u32[]{:S(2)}) copy-start(f32[128]{0:T(128)} %get-tuple-element.77) | copy-start | bytes 1540
  75.8 8.2 %copy-start.15 = (f32[128]{0:T(128)S(1)}, f32[128]{0:T(128)}, u32[]{:S(2)}) copy-start(f32[128]{0:T(128)} %get-tuple-element.78) | copy-start | bytes 1540
  75.8 8.2 %copy-start.16 = (f32[128]{0:T(128)S(1)}, f32[128]{0:T(128)}, u32[]{:S(2)}) copy-start(f32[128]{0:T(128)} %get-tuple-element.79) | copy-start | bytes 1540
  76.0 6.5 %collective-permute-start.4 = (bf16[1,128]{1,0:T(2,128)(2,1)S(1)}, bf16[1,128]{1,0:T(2,128)(2,1)S(1)}, u32[]{:S(2)}, u32[]{:S(2)}) collective-permute-start(bf16[1,128]{1,0:T(2,128)(2,1)S(1)} %get-tuple-element.87), channel_id=1, source_target_pairs={{0,2},{2,4},{4,6},{6,8},{8,10},{10,12},{12,14},{14,16},{16,18},{18... | collective-permute-start | bytes 776 | tf_op jit(solution)/shard_map/ppermute | solution.py:15
  80.8 3.0 %collective-permute-start.5 = (bf16[1,128]{1,0:T(2,128)(2,1)S(1)}, bf16[1,128]{1,0:T(2,128)(2,1)S(1)}, u32[]{:S(2)}, u32[]{:S(2)}) collective-permute-start(bf16[1,128]{1,0:T(2,128)(2,1)S(1)} %get-tuple-element.88), channel_id=1, source_target_pairs={{2,0},{4,2},{6,4},{8,6},{10,8},{12,10},{14,12},{16,14},{18,16},{20... | collective-permute-start | bytes 776 | tf_op jit(solution)/shard_map/ppermute | solution.py:18
  82.4 3.5 %copy-start.7 = (bf16[2,128,128]{1,2,0:T(8,128)(2,1)S(1)}, bf16[2,128,128]{1,2,0:T(8,128)(2,1)}, u32[]{:S(2)}) copy-start(bf16[2,128,128]{1,2,0:T(8,128)(2,1)} %copy-done.6) | copy-start | bytes 196612
  86.6 0.8 copy-start.5
  88.0 0.8 copy-start.3
  (3 other events, 2.0 us)
Sparse Core Ops, SparseCore 0:
  88.9 57.6 reduce-scatter.3
where the time goes:
time: 187 us; the launch traced here: 186 us
  blocking collectives  72.9 us (39%)
  starting transfers between devices  25.2 us (13%)
  waiting for transfers between devices  25.2 us (13%)
  other arithmetic  18.6 us (10%)
  between operations  17.3 us (9%)
  local copies, waits for them, and re-layouts  16.5 us (9%)
  matrix products  10.1 us (5%)
    psum x1, blocking collectives, on_device(): grad_bias, grad_two = lax.psum((grad_bias, grad_two), ('tile', 'rep'))  42.7 us
    all_gather x1, blocking collectives, on_device(): lax.all_gather(share, 'tile', axis=0, tiled=True)  21.1 us
    ppermute x3, starting transfers between devices, extended(): lax.ppermute(lax.slice_in_dim(block, block.shape[dim] - width, None, axis...  10.5 us
    unnamed x2, waiting for transfers between devices  9.84 us
    psum x1, blocking collectives, on_device(): share = lax.psum(share, 'rep')  9.1 us
    all_to_all x1, waiting for transfers between devices, on_device(): lax.all_to_all(send_wave.reshape(tiles, bucket, steps), 'tile', split_axi...  7.75 us
    all_to_all x1, starting transfers between devices, on_device(): lax.all_to_all(send_bin.reshape(tiles, bucket), 'tile', split_axis=0, con...  7.36 us
    add x8, other arithmetic, raster(): wanted = start + jnp.arange(block, dtype=jnp.int32)  5.17 us
  transfers between devices with their start and end apart: 9, of which 6 were waited for; matrix products, arithmetic and copies ran while one was open for 4% of the time, Pallas kernels for 0%

commit v1 on v0

--- a/solution.py
+++ b/solution.py
@@ -128,7 +128,7 @@
     )
     share = lax.psum(share, "rep")
     grad_one = lax.all_gather(share, "tile", axis=0, tiled=True).reshape(3, 3, steps, channels)
-    grad_bias, grad_two = lax.psum((grad_bias, grad_two), ("tile", "rep"))
+    grad_bias, grad_two = lax.psum(lax.psum((grad_bias, grad_two), "rep"), "tile")
     return (pred[None], normalized(grad_one), normalized(grad_bias), normalized(grad_two))
 
 

time: 187 us -> 219 us (1.17)
  waiting for transfers between devices: 25.2 us -> 71 us
  blocking collectives: 72.9 us -> 58.1 us
    unnamed x2, waiting for transfers between devices: 9.84 us -> 55.5 us
    psum x1, blocking collectives: 42.7 us -> 30 us  [on_device(): lax.psum(lax.psum((grad_bias, grad_two), 'rep'), 'tile')]
  transfers between devices with their start and end apart: 9 -> 9, of which waited for: 6 -> 6; matrix products, arithmetic and copies ran while one was open for 4% -> 3% of each run, Pallas kernels for 0% -> 0%
where the time goes in v1:
time: 219 us; the launch traced here: 218 us
  waiting for transfers between devices  71 us (32%)
  blocking collectives  58.1 us (27%)
  starting transfers between devices  25.3 us (12%)
  other arithmetic  18.6 us (8%)
  between operations  17.3 us (8%)
  local copies, waits for them, and re-layouts  17.2 us (8%)
  matrix products  10.1 us (5%)
    unnamed x2, waiting for transfers between devices  55.5 us
    psum x1, blocking collectives, on_device(): lax.psum(lax.psum((grad_bias, grad_two), 'rep'), 'tile')  30 us
    all_gather x1, blocking collectives, on_device(): lax.all_gather(share, 'tile', axis=0, tiled=True)  18.9 us
    ppermute x3, starting transfers between devices, extended(): lax.ppermute(lax.slice_in_dim(block, block.shape[dim] - width, None, axis...  10.5 us
    psum x1, blocking collectives, on_device(): share = lax.psum(share, 'rep')  9.25 us
    all_to_all x1, waiting for transfers between devices, on_device(): lax.all_to_all(send_wave.reshape(tiles, bucket, steps), 'tile', split_axi...  7.75 us
    all_to_all x1, starting transfers between devices, on_device(): lax.all_to_all(send_bin.reshape(tiles, bucket), 'tile', split_axis=0, con...  7.36 us
    add x8, other arithmetic, raster(): wanted = start + jnp.arange(block, dtype=jnp.int32)  5.17 us
  transfers between devices with their start and end apart: 9, of which 6 were waited for; matrix products, arithmetic and copies ran while one was open for 3% of the time, Pallas kernels for 0%

profile of v1, /device:TPU:0, one launch (start us, length us, event | category | flops | bytes accessed | tf_op | source)
XLA Modules:
  0.0 217.9 jit_solution(6169241863647540137)
XLA Ops:
  7.9 1.1 reduce-window.6
  10.8 2.6 %scatter_custom_fusion = s32[512]{0:T(512)S(1)} fusion(s32[512]{0:T(512)S(1)} %bitcast.330, s32[512]{0:T(512)} %bitcast.332, s32[]{:T(128)} %constant.22.clone.1), kind=kCustom, calls=%fused_computation.156 | custom fusion | bytes 2560 | tf_op jit(solution)/shard_map/scatter | solution.py:67
  14.1 7.4 %all-to-all-start = ((s32[16,1,32]{2,1,0:T(1,128)}), s32[16,1,32]{2,1,0:T(1,128)S(1)}, u32[]{:S(2)}, u32[]{:S(2)}) async-start(s32[16,1,32]{2,1,0:T(1,128)} %all_to_all.11), calls=%async_computation | async-start | bytes 16384 | tf_op jit(solution)/shard_map/all_to_all | solution.py:72
  21.4 2.4 %scatter_custom_fusion.1 = bf16[512,128]{1,0:T(8,128)(2,1)} fusion(s32[512]{0:T(512)S(1)} %bitcast.331, bf16[1,512,128]{2,1,0:T(8,128)(2,1)S(1)} %copy-done, bf16[]{:T(256)} %constant.14.clone.1), kind=kCustom, calls=%fused_computation.100 | custom fusion | bytes 262146 | tf_op jit(solution)/shard_map/scatter | solution.py:66
  23.8 4.0 %all-to-all-done = s32[16,1,32]{2,1,0:T(1,128)S(1)} async-done(((s32[16,1,32]{2,1,0:T(1,128)}), s32[16,1,32]{2,1,0:T(1,128)S(1)}, u32[]{:S(2)}, u32[]{:S(2)}) %all-to-all-start) | async-done | bytes 2080 | tf_op jit(solution)/shard_map/all_to_all | solution.py:72
  27.8 3.5 %all-to-all-start.1 = ((bf16[16,32,128]{2,1,0:T(8,128)(2,1)}), bf16[16,32,128]{2,1,0:T(8,128)(2,1)S(1)}, u32[]{:S(2)}, u32[]{:S(2)}) async-start(bf16[16,32,128]{2,1,0:T(8,128)(2,1)} %bitcast.12), calls=%async_computation.1 | async-start | bytes 262144 | tf_op jit(solution)/shard_map/all_to_all | solution.py:69
  31.5 7.8 %all-to-all-done.1 = bf16[16,32,128]{2,1,0:T(8,128)(2,1)S(1)} async-done(((bf16[16,32,128]{2,1,0:T(8,128)(2,1)}), bf16[16,32,128]{2,1,0:T(8,128)(2,1)S(1)}, u32[]{:S(2)}, u32[]{:S(2)}) %all-to-all-start.1) | async-done | bytes 131104 | tf_op jit(solution)/shard_map/all_to_all | solution.py:69
  39.3 12.0 %while.11 = (s32[]{:T(128)}, bf16[8,128,128]{2,1,0:T(8,128)(2,1)S(1)}, s32[8]{0:T(128)S(1)}, s32[16,32]{1,0:T(8,128)}, bf16[512,128]{1,0:T(8,128)(2,1)S(1)}, /*index=5*/s32[512]{0:T(512)S(1)}, s32[]{:T(128)}) while((s32[]{:T(128)}, bf16[8,128,128]{2,1,0:T(8,128)(2,1)S(1)}, s32[8]{0:T(128)S(1)}, s32[16,32]{1,0:T(8,128)}, ...), condition=%wide.wide.region_6.7_spmd, body=%wide.wide.region_5.6_spmd.sunk | while | flops 16859264 | bytes 167009 | solution.py:86
  51.5 1.3 collective-permute-start
  52.8 1.3 collective-permute-start.1
  57.6 0.9 pad_maximum_fusion.2
  61.9 1.0 convolution_add_fusion.8
  65.7 4.4 %collective-permute-start.2 = (bf16[1,128,128]{2,1,0:T(8,128)(2,1)S(1)}, bf16[1,128,128]{2,1,0:T(8,128)(2,1)S(1)}, u32[]{:S(2)}, u32[]{:S(2)}) collective-permute-start(bf16[1,128,128]{2,1,0:T(8,128)(2,1)S(1)} %get-tuple-element.56), channel_id=1, source_target_pairs={{0,2},{2,4},{4,6},{6,8},{8,10},{10,12},{12,14},{14,16},{16,18},{18... | collective-permute-start | bytes 98312 | tf_op jit(solution)/shard_map/ppermute | solution.py:15
  70.1 1.3 collective-permute-start.3
  71.6 1.6 collective-permute-done.3
  76.0 4.8 %collective-permute-start.4 = (bf16[1,128]{1,0:T(2,128)(2,1)S(1)}, bf16[1,128]{1,0:T(2,128)(2,1)S(1)}, u32[]{:S(2)}, u32[]{:S(2)}) collective-permute-start(bf16[1,128]{1,0:T(2,128)(2,1)S(1)} %get-tuple-element.90), channel_id=1, source_target_pairs={{0,2},{2,4},{4,6},{6,8},{8,10},{10,12},{12,14},{14,16},{16,18},{18... | collective-permute-start | bytes 776 | tf_op jit(solution)/shard_map/ppermute | solution.py:15
  80.8 1.3 collective-permute-start.5
  82.3 1.6 collective-permute-done.5
  84.0 1.6 multiply_convert_fusion.1
  89.7 1.6 convert_reduce_fusion
  91.4 55.4 %reduce-scatter.4.cloned.1.call-done = f32[72,128]{1,0:T(8,128)} async-done(((f32[1152,128]{1,0:T(8,128)}), f32[72,128]{1,0:T(8,128)}) %reduce-scatter.4.cloned.1.call-update) | async-done | bytes 36880
  146.8 9.2 %all-reduce.5 = (f32[72,128]{1,0:T(8,128)S(1)}, f32[128]{0:T(128)S(1)}, f32[3,3,128]{2,1,0:T(4,128)S(1)}) all-reduce(f32[72,128]{1,0:T(8,128)} %reduce-scatter.4.cloned.1.call-done, f32[128]{0:T(128)S(1)} %convert_reduce_fusion, f32[3,3,128]{2,1,0:T(4,128)S(1)} %reshape.152), channel_id=1, replica_groups=mesh['tile'=16,'rep'=2] {'rep'}, use_global_device_ids=true, to_apply=%region_8.9 | all-reduce | flops 10496 | bytes 83968 | tf_op jit(solution)/shard_map/psum | solution.py:129
  156.1 30.0 %all-reduce.4 = (f32[128]{0:T(128)S(1)}, f32[3,3,128]{2,1,0:T(4,128)S(1)}) all-reduce(f32[128]{0:T(128)S(1)} %get-tuple-element.45, f32[3,3,128]{2,1,0:T(4,128)S(1)} %get-tuple-element.46), channel_id=1, replica_groups=mesh['tile'=16,'rep'=2] {'tile'}, use_global_device_ids=true, to_apply=%region_12.13 | all-reduce | flops 1280 | bytes 10240 | tf_op jit(solution)/shard_map/psum | solution.py:131
  189.8 18.9 %all_gather.3 = f32[1152,128]{1,0:T(8,128)S(1)} all-gather(f32[72,128]{1,0:T(8,128)S(1)} %get-tuple-element.44), channel_id=1, replica_groups=mesh['tile'=16,'rep'=2] {'tile'}, dimensions={0}, use_global_device_ids=true | all-gather | bytes 626688 | tf_op jit(solution)/shard_map/all_gather | solution.py:130
  (145 shorter events, 35.3 us)
Async XLA Ops:
  7.2 14.3 %copy-start = (bf16[1,512,128]{2,1,0:T(8,128)(2,1)S(1)}, bf16[1,512,128]{2,1,0:T(8,128)(2,1)}, u32[]{:S(2)}) copy-start(bf16[1,512,128]{2,1,0:T(8,128)(2,1)} %param.10) | copy-start | bytes 393220
  14.1 13.8 %all-to-all-start = ((s32[16,1,32]{2,1,0:T(1,128)}), s32[16,1,32]{2,1,0:T(1,128)S(1)}, u32[]{:S(2)}, u32[]{:S(2)}) async-start(s32[16,1,32]{2,1,0:T(1,128)} %all_to_all.11), calls=%async_computation | async-start | bytes 16384 | tf_op jit(solution)/shard_map/all_to_all | solution.py:72
  27.8 11.4 %copy-start.10 = (s32[16,1,32]{2,1,0:T(1,128)}, s32[16,1,32]{2,1,0:T(1,128)S(1)}, u32[]{:S(2)}) copy-start(s32[16,1,32]{2,1,0:T(1,128)S(1)} %all-to-all-done) | copy-start | bytes 6148
  27.8 11.4 %all-to-all-start.1 = ((bf16[16,32,128]{2,1,0:T(8,128)(2,1)}), bf16[16,32,128]{2,1,0:T(8,128)(2,1)S(1)}, u32[]{:S(2)}, u32[]{:S(2)}) async-start(bf16[16,32,128]{2,1,0:T(8,128)(2,1)} %bitcast.12), calls=%async_computation.1 | async-start | bytes 262144 | tf_op jit(solution)/shard_map/all_to_all | solution.py:69
  31.4 115.5 %reduce-scatter.4.cloned.1.call-start = ((), (), s32[]{:S(2)}) async-start(), calls=%async_computation.3 | async-start | bytes 626688
  39.3 14.9 %copy-start.11 = (bf16[3,3,128]{2,1,0:T(4,128)(2,1)S(1)}, bf16[3,3,128]{2,1,0:T(4,128)(2,1)}, u32[]{:S(2)}) copy-start(bf16[3,3,128]{2,1,0:T(4,128)(2,1)} %param.16) | copy-start | bytes 6916
  51.5 3.9 %collective-permute-start = (bf16[2,128,128]{1,2,0:T(8,128)(2,1)S(1)}, bf16[2,128,128]{1,2,0:T(8,128)(2,1)S(1)}, u32[]{:S(2)}, u32[]{:S(2)}) collective-permute-start(bf16[2,128,128]{1,2,0:T(8,128)(2,1)S(1)} %get-tuple-element.60), channel_id=1, source_target_pairs={{0,2},{2,4},{4,6},{6,8},{8,10},{10,12},{12,14},{14,16},{16,18},{18... | collective-permute-start | bytes 196616 | tf_op jit(solution)/shard_map/ppermute | solution.py:15
  52.8 3.1 %collective-permute-start.1 = (bf16[2,128,128]{1,2,0:T(8,128)(2,1)S(1)}, bf16[2,128,128]{1,2,0:T(8,128)(2,1)S(1)}, u32[]{:S(2)}, u32[]{:S(2)}) collective-permute-start(bf16[2,128,128]{1,2,0:T(8,128)(2,1)S(1)} %get-tuple-element.61), channel_id=1, source_target_pairs={{2,0},{4,2},{6,4},{8,6},{10,8},{12,10},{14,12},{16,14},{18,16},{20... | collective-permute-start | bytes 196616 | tf_op jit(solution)/shard_map/ppermute | solution.py:18
  61.6 1.3 copy-start.3
  61.8 1.1 copy-start.9
  62.9 1.0 copy-start.2
  63.2 1.0 copy-start.1
  65.7 5.9 %collective-permute-start.2 = (bf16[1,128,128]{2,1,0:T(8,128)(2,1)S(1)}, bf16[1,128,128]{2,1,0:T(8,128)(2,1)S(1)}, u32[]{:S(2)}, u32[]{:S(2)}) collective-permute-start(bf16[1,128,128]{2,1,0:T(8,128)(2,1)S(1)} %get-tuple-element.56), channel_id=1, source_target_pairs={{0,2},{2,4},{4,6},{6,8},{8,10},{10,12},{12,14},{14,16},{16,18},{18... | collective-permute-start | bytes 98312 | tf_op jit(solution)/shard_map/ppermute | solution.py:15
  70.1 3.1 %collective-permute-start.3 = (bf16[1,128,128]{2,1,0:T(8,128)(2,1)S(1)}, bf16[1,128,128]{2,1,0:T(8,128)(2,1)S(1)}, u32[]{:S(2)}, u32[]{:S(2)}) collective-permute-start(bf16[1,128,128]{2,1,0:T(8,128)(2,1)S(1)} %get-tuple-element.57), channel_id=1, source_target_pairs={{2,0},{4,2},{6,4},{8,6},{10,8},{12,10},{14,12},{16,14},{18,16},{20... | collective-permute-start | bytes 98312 | tf_op jit(solution)/shard_map/ppermute | solution.py:18
  75.5 8.5 %copy-start.12 = (f32[128]{0:T(128)S(1)}, f32[128]{0:T(128)}, u32[]{:S(2)}) copy-start(f32[128]{0:T(128)} %get-tuple-element.77) | copy-start | bytes 1540
  75.5 8.5 %copy-start.13 = (f32[128]{0:T(128)S(1)}, f32[128]{0:T(128)}, u32[]{:S(2)}) copy-start(f32[128]{0:T(128)} %get-tuple-element.78) | copy-start | bytes 1540
  75.5 8.5 %copy-start.14 = (f32[128]{0:T(128)S(1)}, f32[128]{0:T(128)}, u32[]{:S(2)}) copy-start(f32[128]{0:T(128)} %get-tuple-element.79) | copy-start | bytes 1540
  75.5 8.5 %copy-start.15 = (f32[128]{0:T(128)S(1)}, f32[128]{0:T(128)}, u32[]{:S(2)}) copy-start(f32[128]{0:T(128)} %get-tuple-element.80) | copy-start | bytes 1540
  75.5 8.5 %copy-start.16 = (f32[128]{0:T(128)S(1)}, f32[128]{0:T(128)}, u32[]{:S(2)}) copy-start(f32[128]{0:T(128)} %get-tuple-element.81) | copy-start | bytes 1540
  75.6 8.5 %copy-start.17 = (f32[128]{0:T(128)S(1)}, f32[128]{0:T(128)}, u32[]{:S(2)}) copy-start(f32[128]{0:T(128)} %get-tuple-element.82) | copy-start | bytes 1540
  76.0 6.2 %collective-permute-start.4 = (bf16[1,128]{1,0:T(2,128)(2,1)S(1)}, bf16[1,128]{1,0:T(2,128)(2,1)S(1)}, u32[]{:S(2)}, u32[]{:S(2)}) collective-permute-start(bf16[1,128]{1,0:T(2,128)(2,1)S(1)} %get-tuple-element.90), channel_id=1, source_target_pairs={{0,2},{2,4},{4,6},{6,8},{8,10},{10,12},{12,14},{14,16},{16,18},{18... | collective-permute-start | bytes 776 | tf_op jit(solution)/shard_map/ppermute | solution.py:15
  80.8 3.0 %collective-permute-start.5 = (bf16[1,128]{1,0:T(2,128)(2,1)S(1)}, bf16[1,128]{1,0:T(2,128)(2,1)S(1)}, u32[]{:S(2)}, u32[]{:S(2)}) collective-permute-start(bf16[1,128]{1,0:T(2,128)(2,1)S(1)} %get-tuple-element.91), channel_id=1, source_target_pairs={{2,0},{4,2},{6,4},{8,6},{10,8},{12,10},{14,12},{16,14},{18,16},{20... | collective-permute-start | bytes 776 | tf_op jit(solution)/shard_map/ppermute | solution.py:18
  82.2 3.6 %copy-start.8 = (bf16[2,128,128]{1,2,0:T(8,128)(2,1)S(1)}, bf16[2,128,128]{1,2,0:T(8,128)(2,1)}, u32[]{:S(2)}) copy-start(bf16[2,128,128]{1,2,0:T(8,128)(2,1)} %copy-done.7) | copy-start | bytes 196612
  86.6 0.8 copy-start.6
  (5 other events, 3.4 us)
Sparse Core Ops, SparseCore 0:
  89.0 57.8 reduce-scatter.3
